TPU v7x, 32 devices: a whole 2x2x4 slice. The times are simulated.
32 devices in a mesh: ctx: 16 (over z, x, core), chan: 2 (over y).
Axes of the slice: x: 2, y: 2, z: 4, core: 2. Of those that a mesh axis runs over, the one named last changes fastest.
Arguments:
- query_act: bfloat16 [2048, 1024], P('ctx', 'chan'), may hold values from -6 to 6
- key_act: bfloat16 [2048, 1024], P('ctx', 'chan'), may hold values from -6 to 6
- value_act: bfloat16 [2048, 1024], P('ctx', 'chan'), may hold values from -6 to 6
- filters: bfloat16 [2048, 1024], P('ctx', 'chan'), may hold values from -0.125 to 0.125
- skip_scale: float32 [1024], P('chan'), may hold values from -4 to 4
- w_out: bfloat16 [1024, 4096], P('chan'), may hold values from -0.25 to 0.25
Outputs:
- projected: bfloat16 [2048, 4096], P('ctx', 'chan')
All inputs are finite; a program needn't handle non-finite values.
Results may differ from a plain program's by a relative error of at most 0.015.
Values may be sent and summed in bfloat16 or wider, within the bound.
A program may use at most 64 MiB of HBM per device.

v0:
```python
import math

import jax
import jax.numpy as jnp
from jax import lax
from jax.sharding import PartitionSpec as P

precise = lax.Precision.HIGHEST


def phase_table(row_count, col_count, modulus, factor):
    row_index = lax.broadcasted_iota(jnp.int32, (row_count, col_count), 0)
    col_index = lax.broadcasted_iota(jnp.int32, (row_count, col_count), 1)
    phase_angle = (row_index * col_index % modulus).astype(jnp.float32) * (2.0 * math.pi / modulus)
    return (jnp.cos(phase_angle) * factor, jnp.sin(phase_angle) * factor)


def twiddle(freq_index, pos_index, modulus):
    phase_angle = (freq_index * pos_index % modulus).astype(jnp.float32) * (2.0 * math.pi / modulus)
    return (jnp.cos(phase_angle), jnp.sin(phase_angle))


def shards(query_act, key_act, value_act, filters, skip_scale, w_out):
    tok_rows, chan_width = key_act.shape
    ctx_size = lax.axis_size("ctx")
    per_dev = tok_rows // ctx_size
    fft_length = 2 * tok_rows * ctx_size
    freq_blocks = 2 * ctx_size
    ctx_index = lax.axis_index("ctx")
    gated_in = (key_act.astype(jnp.float32) * value_act.astype(jnp.float32)).astype(jnp.bfloat16)
    sent_input, sent_filter = (
        lax.all_to_all(
            gated_in.reshape(1, ctx_size, per_dev, chan_width),
            "ctx",
            split_axis=1,
            concat_axis=0,
            tiled=True,
        ),
        lax.all_to_all(
            filters.reshape(1, ctx_size, per_dev, chan_width),
            "ctx",
            split_axis=1,
            concat_axis=0,
            tiled=True,
        ),
    )
    block_cos, block_sin = phase_table(freq_blocks, ctx_size, freq_blocks, 1.0)
    offsets = ctx_index * per_dev + lax.broadcasted_iota(jnp.int32, (1, per_dev), 1)
    all_freq = lax.broadcasted_iota(jnp.int32, (freq_blocks, 1), 0)
    front_cos, front_sin = twiddle(all_freq, offsets, fft_length)
    front_cos = front_cos[:, :, None]
    front_sin = front_sin[:, :, None]

    def first_section(signal):
        values32 = signal.reshape(ctx_size, per_dev, chan_width).astype(jnp.float32)
        real_part = jnp.einsum("kp,pjc->kjc", block_cos, values32, precision=precise)
        imag_part = -jnp.einsum("kp,pjc->kjc", block_sin, values32, precision=precise)
        out_real = real_part * front_cos + imag_part * front_sin
        out_imag = imag_part * front_cos - real_part * front_sin
        return jnp.stack([out_real, out_imag]).reshape(2, ctx_size, 2, per_dev, chan_width)

    cycle_cos, cycle_sin = phase_table(tok_rows, tok_rows, tok_rows, 1.0)

    def cycle_apply(table, operand):
        return jnp.einsum("kn,zmnc->zmkc", table, operand, precision=precise)

    spec_input = lax.all_to_all(
        first_section(sent_input), "ctx", split_axis=1, concat_axis=3, tiled=True
    )
    spec_filter = lax.all_to_all(
        first_section(sent_filter), "ctx", split_axis=1, concat_axis=3, tiled=True
    )

    def forward(portion):
        real_in = portion[0]
        imag_in = portion[1]
        out_real = cycle_apply(cycle_cos, real_in) + cycle_apply(cycle_sin, imag_in)
        out_imag = cycle_apply(cycle_cos, imag_in) - cycle_apply(cycle_sin, real_in)
        return (out_real, out_imag)

    input_real, input_imag = forward(spec_input)
    filter_real, filter_imag = forward(spec_filter)
    prod_real = input_real * filter_real - input_imag * filter_imag
    prod_imag = input_real * filter_imag + input_imag * filter_real
    back_real = cycle_apply(cycle_cos, prod_real) - cycle_apply(cycle_sin, prod_imag)
    back_imag = cycle_apply(cycle_cos, prod_imag) + cycle_apply(cycle_sin, prod_real)
    mixed = jnp.stack([back_real, back_imag])
    inverted = mixed[:, 0]
    pack_width = inverted.shape[-1]
    own_freq = 2 * ctx_index + lax.broadcasted_iota(jnp.int32, (2, 1), 0)
    all_offsets = lax.broadcasted_iota(jnp.int32, (1, tok_rows), 1)
    back_cos, back_sin = twiddle(own_freq, all_offsets, fft_length)
    back_cos = back_cos[:, :, None]
    back_sin = back_sin[:, :, None]
    turned_real = inverted[0] * back_cos - inverted[1] * back_sin
    turned_imag = inverted[0] * back_sin + inverted[1] * back_cos
    turned = jnp.stack([turned_real, turned_imag]).reshape(2, 2, ctx_size, per_dev, pack_width)
    last_cos, last_sin = phase_table(ctx_size, freq_blocks, freq_blocks, 1.0 / fft_length)

    def last_apply(table, operand):
        return jnp.einsum("nk,kzmc->nzmc", table, operand, precision=precise)

    portion = lax.all_to_all(turned, "ctx", split_axis=2, concat_axis=1, tiled=True)
    returned = last_apply(last_cos, portion[0]) - last_apply(last_sin, portion[1])
    convolved = lax.all_to_all(returned, "ctx", split_axis=0, concat_axis=1, tiled=True).reshape(
        tok_rows, chan_width
    )
    gated = (
        query_act.astype(jnp.float32)
        * (convolved + skip_scale[None, :] * gated_in.astype(jnp.float32))
    ).astype(jnp.bfloat16)
    summed = lax.psum_scatter(
        lax.dot_general(
            w_out, gated, (((0,), (1,)), ((), ())), preferred_element_type=jnp.float32
        ).astype(jnp.bfloat16),
        "chan",
        scatter_dimension=0,
        tiled=True,
    )
    return summed.T


def solution(mesh):
    return jax.shard_map(
        shards,
        mesh=mesh,
        in_specs=(
            P("ctx", "chan"),
            P("ctx", "chan"),
            P("ctx", "chan"),
            P("ctx", "chan"),
            P("chan"),
            P("chan", None),
        ),
        out_specs=P("ctx", "chan"),
        check_vma=False,
    )
```

profile of v0, /device:TPU:0, one launch (start us, length us, event | category | flops | bytes accessed | tf_op | source)
XLA Modules:
  0.0 180.7 jit_solution(6431051070737040364)
XLA Ops:
  6.5 1.7 fusion.49
  8.2 7.4 %all-to-all-start = ((bf16[1,16,8,512]{3,2,0,1:T(8,128)(2,1)}), bf16[1,16,8,512]{3,2,0,1:T(8,128)(2,1)S(1)}, u32[]{:S(2)}, u32[]{:S(2)}) async-start(bf16[1,16,8,512]{3,2,0,1:T(8,128)(2,1)} %fusion.49), calls=%async_computation | async-start | bytes 262144 | tf_op jit(solution)/shard_map/all_to_all | solution.py:32
  15.6 0.1 fusion.103
  15.7 7.8 %all-to-all-done = bf16[1,16,8,512]{3,2,0,1:T(8,128)(2,1)S(1)} async-done(((bf16[1,16,8,512]{3,2,0,1:T(8,128)(2,1)}), bf16[1,16,8,512]{3,2,0,1:T(8,128)(2,1)S(1)}, u32[]{:S(2)}, u32[]{:S(2)}) %all-to-all-start) | async-done | bytes 131104 | tf_op jit(solution)/shard_map/all_to_all | solution.py:32
  23.5 3.5 %all-to-all-start.2 = ((bf16[1,16,8,512]{3,2,0,1:T(8,128)(2,1)}), bf16[1,16,8,512]{3,2,0,1:T(8,128)(2,1)S(1)}, u32[]{:S(2)}, u32[]{:S(2)}) async-start(bf16[1,16,8,512]{3,2,0,1:T(8,128)(2,1)} %bitcast.166), calls=%async_computation.2 | async-start | bytes 262144 | tf_op jit(solution)/shard_map/all_to_all | solution.py:39
  27.0 0.5 convolution_negate_fusion.1
  27.5 0.5 fusion.24
  28.0 6.9 %all-to-all-done.2 = bf16[1,16,8,512]{3,2,0,1:T(8,128)(2,1)S(1)} async-done(((bf16[1,16,8,512]{3,2,0,1:T(8,128)(2,1)}), bf16[1,16,8,512]{3,2,0,1:T(8,128)(2,1)S(1)}, u32[]{:S(2)}, u32[]{:S(2)}) %all-to-all-start.2) | async-done | bytes 131104 | tf_op jit(solution)/shard_map/all_to_all | solution.py:39
  34.9 0.5 fusion.21
  35.4 0.6 multiply_add_fusion.1
  36.0 0.3 copy.79
  36.4 0.3 copy.80
  36.7 1.1 pad_maximum_fusion.1
  37.8 3.7 %all-to-all-start.3 = ((f32[2,16,2,8,512]{4,3,2,0,1:T(8,128)}), f32[2,16,2,8,512]{4,3,2,0,1:T(8,128)S(1)}, u32[]{:S(2)}, u32[]{:S(2)}) async-start(f32[2,16,2,8,512]{4,3,2,0,1:T(8,128)} %pad_maximum_fusion.1), calls=%async_computation.3 | async-start | bytes 2097152 | tf_op jit(solution)/shard_map/all_to_all | solution.py:70
  41.4 0.3 copy.78
  41.7 0.3 copy.77
  42.1 1.1 pad_maximum_fusion
  43.1 21.2 %all-to-all-done.3 = f32[2,16,2,8,512]{4,3,2,0,1:T(8,128)S(1)} async-done(((f32[2,16,2,8,512]{4,3,2,0,1:T(8,128)}), f32[2,16,2,8,512]{4,3,2,0,1:T(8,128)S(1)}, u32[]{:S(2)}, u32[]{:S(2)}) %all-to-all-start.3) | async-done | bytes 1048608 | tf_op jit(solution)/shard_map/all_to_all | solution.py:70
  64.3 6.8 %all-to-all-start.1 = ((f32[2,16,2,8,512]{4,3,2,0,1:T(8,128)}), f32[2,16,2,8,512]{4,3,2,0,1:T(8,128)S(1)}, u32[]{:S(2)}, u32[]{:S(2)}) async-start(f32[2,16,2,8,512]{4,3,2,0,1:T(8,128)} %pad_maximum_fusion), calls=%async_computation.1 | async-start | bytes 2097152 | tf_op jit(solution)/shard_map/all_to_all | solution.py:67
  71.1 0.2 reduce-scatter.2.cloned.1.call-start
  71.4 0.1 fusion.108
  71.5 0.1 copy.108
  71.6 1.1 fusion.16
  72.7 1.1 fusion.15
  73.8 20.2 %all-to-all-done.1 = f32[2,16,2,8,512]{4,3,2,0,1:T(8,128)S(1)} async-done(((f32[2,16,2,8,512]{4,3,2,0,1:T(8,128)}), f32[2,16,2,8,512]{4,3,2,0,1:T(8,128)S(1)}, u32[]{:S(2)}, u32[]{:S(2)}) %all-to-all-start.1) | async-done | bytes 1048608 | tf_op jit(solution)/shard_map/all_to_all | solution.py:67
  94.1 0.1 copy.109
  94.2 1.1 fusion.14
  95.3 1.1 fusion.13
  96.4 1.1 convolution_subtract_fusion.1
  97.5 1.1 convolution_add_fusion.1
  98.7 1.1 convolution_add_fusion.2
  99.8 1.1 multiply_subtract_fusion
  100.9 0.9 fusion.8
  101.8 0.9 fusion.10
  102.7 0.9 fusion.1
  103.6 1.2 subtract_bitcast_fusion
  104.8 0.1 pad_maximum_fusion.2
  104.9 0.0 copy-start
  104.9 0.0 copy-start.1
  104.9 0.0 copy-start.2
  104.9 0.0 copy-start.3
  105.0 0.0 copy-start.4
  105.0 0.1 copy.81
  105.1 31.8 %all_to_all.72 = f32[2,2,16,8,512]{4,3,1,0,2:T(8,128)S(1)} all-to-all(f32[2,2,16,8,512]{4,3,1,0,2:T(8,128)S(1)} %copy.81), channel_id=1, replica_groups=mesh['ctx'=16,'chan'=2] {'ctx'}, dimensions={2} | all-to-all | bytes 2097152 | tf_op jit(solution)/shard_map/all_to_all | solution.py:103
  136.8 0.1 fusion.183
  136.9 0.7 fusion.5
  137.6 0.7 fusion.3
  138.3 0.2 copy.64
  138.5 14.8 %all_to_all.73 = f32[16,1,8,512]{3,2,1,0:T(8,128)S(1)} all-to-all(f32[16,1,8,512]{3,2,1,0:T(8,128)S(1)} %copy.64), channel_id=1, replica_groups=mesh['ctx'=16,'chan'=2] {'ctx'}, dimensions={0} | all-to-all | bytes 524288 | tf_op jit(solution)/shard_map/all_to_all | solution.py:105
  153.3 0.0 copy-done
  153.3 0.0 copy-done.1
  153.3 0.0 copy-done.2
  153.3 0.0 copy-done.3
  153.3 0.0 copy-done.4
  153.3 1.7 fusion
  155.0 0.0 reduce-scatter.2.cloned.1.call-update
  155.1 18.8 %reduce-scatter.2.cloned.1.call-done = bf16[2048,128]{0,1:T(8,128)(2,1)} async-done(((bf16[4096,128]{0,1:T(8,128)(2,1)}), bf16[2048,128]{0,1:T(8,128)(2,1)}) %reduce-scatter.2.cloned.1.call-update) | async-done | bytes 524304 | tf_op jit(solution)/shard_map/reduce_scatter | solution.py:112
  (2 shorter events, 0.0 us)
Async XLA Ops:
  8.2 15.3 %all-to-all-start = ((bf16[1,16,8,512]{3,2,0,1:T(8,128)(2,1)}), bf16[1,16,8,512]{3,2,0,1:T(8,128)(2,1)S(1)}, u32[]{:S(2)}, u32[]{:S(2)}) async-start(bf16[1,16,8,512]{3,2,0,1:T(8,128)(2,1)} %fusion.49), calls=%async_computation | async-start | bytes 262144 | tf_op jit(solution)/shard_map/all_to_all | solution.py:32
  23.5 11.4 %all-to-all-start.2 = ((bf16[1,16,8,512]{3,2,0,1:T(8,128)(2,1)}), bf16[1,16,8,512]{3,2,0,1:T(8,128)(2,1)S(1)}, u32[]{:S(2)}, u32[]{:S(2)}) async-start(bf16[1,16,8,512]{3,2,0,1:T(8,128)(2,1)} %bitcast.166), calls=%async_computation.2 | async-start | bytes 262144 | tf_op jit(solution)/shard_map/all_to_all | solution.py:39
  37.8 26.6 %all-to-all-start.3 = ((f32[2,16,2,8,512]{4,3,2,0,1:T(8,128)}), f32[2,16,2,8,512]{4,3,2,0,1:T(8,128)S(1)}, u32[]{:S(2)}, u32[]{:S(2)}) async-start(f32[2,16,2,8,512]{4,3,2,0,1:T(8,128)} %pad_maximum_fusion.1), calls=%async_computation.3 | async-start | bytes 2097152 | tf_op jit(solution)/shard_map/all_to_all | solution.py:70
  64.3 29.8 %all-to-all-start.1 = ((f32[2,16,2,8,512]{4,3,2,0,1:T(8,128)}), f32[2,16,2,8,512]{4,3,2,0,1:T(8,128)S(1)}, u32[]{:S(2)}, u32[]{:S(2)}) async-start(f32[2,16,2,8,512]{4,3,2,0,1:T(8,128)} %pad_maximum_fusion), calls=%async_computation.1 | async-start | bytes 2097152 | tf_op jit(solution)/shard_map/all_to_all | solution.py:67
  71.1 102.7 %reduce-scatter.2.cloned.1.call-start = ((), (), s32[]{:S(2)}) async-start(), calls=%async_computation.7 | async-start | bytes 1572864 | tf_op jit(solution)/shard_map/reduce_scatter | solution.py:112
  104.9 48.4 %copy-start = (bf16[512,4096]{1,0:T(8,128)(2,1)S(1)}, bf16[512,4096]{1,0:T(8,128)(2,1)}, u32[]{:S(2)}) copy-start(bf16[512,4096]{1,0:T(8,128)(2,1)} %param.11) | copy-start | bytes 12582916
  104.9 48.4 %copy-start.1 = (bf16[128,512]{1,0:T(8,128)(2,1)S(1)}, bf16[128,512]{1,0:T(8,128)(2,1)}, u32[]{:S(2)}) copy-start(bf16[128,512]{1,0:T(8,128)(2,1)} %param.8) | copy-start | bytes 393220
  104.9 48.4 %copy-start.2 = (bf16[128,512]{1,0:T(8,128)(2,1)S(1)}, bf16[128,512]{1,0:T(8,128)(2,1)}, u32[]{:S(2)}) copy-start(bf16[128,512]{1,0:T(8,128)(2,1)} %param.7) | copy-start | bytes 393220
  104.9 48.4 %copy-start.3 = (bf16[128,512]{1,0:T(8,128)(2,1)S(1)}, bf16[128,512]{1,0:T(8,128)(2,1)}, u32[]{:S(2)}) copy-start(bf16[128,512]{1,0:T(8,128)(2,1)} %param.6) | copy-start | bytes 393220
  105.0 48.4 %copy-start.4 = (f32[512]{0:T(512)S(1)}, f32[512]{0:T(512)}, u32[]{:S(2)}) copy-start(f32[512]{0:T(512)} %param.10) | copy-start | bytes 6148
Sparse Core Ops, SparseCore 0:
  155.2 18.6 reduce-scatter.1
where the time goes:
time: 181 us
  waiting for transfers between devices  75 us (41%)
  blocking collectives  46.6 us (26%)
  starting transfers between devices  21.6 us (12%)
  matrix products  17.9 us (10%)
  between operations  13.7 us (8%)
  other arithmetic  4.15 us (2%)
    all_to_all x1, blocking collectives, shards(): lax.all_to_all(turned, 'ctx', split_axis=2, concat_axis=1, tiled=True)  31.8 us
    all_to_all x1, waiting for transfers between devices, shards(): lax.all_to_all(first_section(sent_filter), 'ctx', split_axis=1, concat_ax...  21.2 us
    all_to_all x1, waiting for transfers between devices, shards(): lax.all_to_all(first_section(sent_input), 'ctx', split_axis=1, concat_axi...  20.2 us
    reduce_scatter x1, waiting for transfers between devices, shards(): lax.psum_scatter(lax.dot_general(w_out, gated, (((0,), (1,)), ((), ())),...  18.8 us
    all_to_all x1, blocking collectives, shards(): lax.all_to_all(returned, 'ctx', split_axis=0, concat_axis=1, tiled=True)  14.8 us
    dot_general x12, matrix products, cycle_apply(): return jnp.einsum('kn,zmnc->zmkc', table, operand, precision=precise)  12.8 us
    all_to_all x1, waiting for transfers between devices, shards(): lax.all_to_all(gated_in.reshape(1, ctx_size, per_dev, chan_width), 'ctx',...  7.8 us
    all_to_all x1, starting transfers between devices, shards(): lax.all_to_all(gated_in.reshape(1, ctx_size, per_dev, chan_width), 'ctx',...  7.36 us
  transfers between devices with their start and end apart: 5, of which 5 were waited for; matrix products, arithmetic and copies ran while one was open for 3% of the time, Pallas kernels for 0%

commit v1 on v0

v1 whole, which is shorter than its diff:
```python
import functools
import math

import jax
import jax.numpy as jnp
import numpy as np
from jax import lax
from jax.experimental import pallas as pl
from jax.experimental.pallas import tpu as pltpu
from jax.sharding import PartitionSpec as P

MESH = pl.DeviceIdType.MESH
TILE = 8


def tables(block):
    pos = np.arange(block)
    angle = 2.0 * math.pi * np.outer(pos, pos + 0.25) / block
    forward = np.concatenate([np.cos(angle), -np.sin(angle)], axis=1)
    cos, sin = np.cos(angle).T / block, np.sin(angle).T / block
    inverse = np.block([[cos, -sin], [-sin, -cos]])
    return jnp.asarray(forward, jnp.bfloat16), jnp.asarray(inverse, jnp.bfloat16)


def kernel(
    n_ctx, n_chan, chunk,
    query_ref, key_ref, value_ref, filter_ref, skip_ref, fwd_ref, inv_ref, w_ref,
    out_ref,
    send, recv, spec, prod, back_send, back_recv, w_vmem, part_send, part_recv, own_part,
    send_sem, recv_sem, back_send_sem, back_recv_sem, part_send_sem, part_recv_sem, w_sem,
):
    me = lax.axis_index("ctx")
    my_chan = lax.axis_index("chan")
    block, width = key_ref.shape
    chans = width // n_ctx
    groups = chans // TILE
    feats = out_ref.shape[1]
    chunks = feats // chunk

    barrier = pltpu.get_barrier_semaphore()

    @pl.loop(1, n_ctx)
    def _(step):
        pl.semaphore_signal(barrier, inc=1, device_id={"ctx": lax.rem(me + step, n_ctx)}, device_id_type=MESH)

    @pl.loop(1, n_chan)
    def _(step):
        pl.semaphore_signal(barrier, inc=1, device_id={"chan": lax.rem(my_chan + step, n_chan)}, device_id_type=MESH)

    w_copy = pltpu.make_async_copy(w_ref, w_vmem, w_sem)
    w_copy.start()

    gated_in = (key_ref[...].astype(jnp.float32) * value_ref[...].astype(jnp.float32)).astype(jnp.bfloat16).astype(jnp.float32)
    signal_t = gated_in.T.reshape(n_ctx, chans, block)
    filter_t = filter_ref[...].astype(jnp.float32).T.reshape(n_ctx, chans, block)
    send[...] = jnp.concatenate([signal_t, filter_t], axis=1).astype(jnp.bfloat16)

    pl.semaphore_wait(barrier, n_ctx + n_chan - 2)

    def out_copy(peer):
        return pltpu.make_async_remote_copy(
            src_ref=send.at[peer], dst_ref=recv.at[me],
            send_sem=send_sem.at[peer], recv_sem=recv_sem.at[me],
            device_id={"ctx": peer}, device_id_type=MESH)

    def in_copy(peer):
        return pltpu.make_async_remote_copy(
            src_ref=send.at[me], dst_ref=recv.at[peer],
            send_sem=send_sem.at[me], recv_sem=recv_sem.at[peer],
            device_id={"ctx": peer}, device_id_type=MESH)

    @pl.loop(1, n_ctx)
    def _(step):
        out_copy(lax.rem(me + step, n_ctx)).start()

    recv[me] = send[me]

    @pl.loop(1, n_ctx)
    def _(step):
        in_copy(lax.rem(me + step, n_ctx)).wait_recv()

    spec[...] = jnp.dot(
        recv[...].reshape(n_ctx * 2 * chans, block), fwd_ref[...], preferred_element_type=jnp.float32
    ).reshape(n_ctx, 2 * groups, TILE, 2 * block)

    low, high = pl.ds(0, block), pl.ds(block, block)

    @pl.loop(0, groups)
    def _(group):
        @pl.loop(0, n_ctx // TILE)
        def _(tile):
            def accumulate(first, lag, acc, diagonal):
                acc = list(acc)
                lags = {}
                for i in range(0 if diagonal else 1 - TILE, TILE):
                    lags[i] = (spec[lag + i, groups + group, :, low], spec[lag + i, groups + group, :, high])
                for j in range(TILE):
                    real, imag = spec[first + j, group, :, low], spec[first + j, group, :, high]
                    for i in range(j if diagonal else 0, TILE):
                        f_real, f_imag = lags[i - j]
                        acc[2 * i] = acc[2 * i] + (real * f_real - imag * f_imag)
                        acc[2 * i + 1] = acc[2 * i + 1] + (real * f_imag + imag * f_real)
                return tuple(acc)

            zero = jnp.zeros((TILE, block), jnp.float32)
            acc = accumulate(tile * TILE, 0, (zero,) * (2 * TILE), True)
            acc = lax.fori_loop(
                0, tile, lambda u, acc: accumulate(u * TILE, (tile - u) * TILE, acc, False), acc)
            for i in range(TILE):
                prod[tile * TILE + i, group, :, low] = acc[2 * i]
                prod[tile * TILE + i, group, :, high] = acc[2 * i + 1]

    mixed = jnp.dot(
        prod[...].reshape(n_ctx * chans, 2 * block).astype(jnp.bfloat16), inv_ref[...],
        preferred_element_type=jnp.float32)
    first, carry = mixed[:, :block], mixed[:, block:]
    shifted = jnp.concatenate([jnp.zeros((chans, block), jnp.float32), carry[:-chans]], axis=0)
    back_send[...] = (first + shifted).reshape(n_ctx, chans, block).astype(jnp.bfloat16)

    def back_out(peer):
        return pltpu.make_async_remote_copy(
            src_ref=back_send.at[peer], dst_ref=back_recv.at[me],
            send_sem=back_send_sem.at[peer], recv_sem=back_recv_sem.at[me],
            device_id={"ctx": peer}, device_id_type=MESH)

    def back_in(peer):
        return pltpu.make_async_remote_copy(
            src_ref=back_send.at[me], dst_ref=back_recv.at[peer],
            send_sem=back_send_sem.at[me], recv_sem=back_recv_sem.at[peer],
            device_id={"ctx": peer}, device_id_type=MESH)

    @pl.loop(1, n_ctx)
    def _(step):
        back_out(lax.rem(me + step, n_ctx)).start()

    back_recv[me] = back_send[me]
    w_copy.wait()

    @pl.loop(1, n_ctx)
    def _(step):
        back_in(lax.rem(me + step, n_ctx)).wait_recv()

    convolved = back_recv[...].astype(jnp.float32).reshape(width, block).T
    signal = (key_ref[...].astype(jnp.float32) * value_ref[...].astype(jnp.float32)).astype(jnp.bfloat16).astype(jnp.float32)
    gated = (query_ref[...].astype(jnp.float32) * (convolved + skip_ref[...] * signal)).astype(jnp.bfloat16)

    def product(chan, piece):
        columns = pl.ds(pl.multiple_of(chan * feats + piece * chunk, chunk), chunk)
        return jnp.dot(gated, w_vmem[:, columns], preferred_element_type=jnp.float32)

    def part_out(chan, piece):
        return pltpu.make_async_remote_copy(
            src_ref=part_send.at[chan, piece], dst_ref=part_recv.at[my_chan, piece],
            send_sem=part_send_sem.at[chan, piece], recv_sem=part_recv_sem.at[my_chan, piece],
            device_id={"chan": chan}, device_id_type=MESH)

    def part_in(chan, piece):
        return pltpu.make_async_remote_copy(
            src_ref=part_send.at[my_chan, piece], dst_ref=part_recv.at[chan, piece],
            send_sem=part_send_sem.at[my_chan, piece], recv_sem=part_recv_sem.at[chan, piece],
            device_id={"chan": chan}, device_id_type=MESH)

    @pl.loop(1, n_chan)
    def _(step):
        chan = lax.rem(my_chan + step, n_chan)

        @pl.loop(0, chunks)
        def _(piece):
            part_send[chan, piece] = product(chan, piece).astype(jnp.bfloat16)
            part_out(chan, piece).start()

    @pl.loop(0, chunks)
    def _(piece):
        own_part[piece] = product(my_chan, piece).astype(jnp.bfloat16).astype(jnp.float32)

    for piece in range(chunks):
        def add(step, total):
            chan = lax.rem(my_chan + step, n_chan)
            part_in(chan, piece).wait_recv()
            return total + part_recv[chan, piece].astype(jnp.float32)
        out_ref[:, piece * chunk:(piece + 1) * chunk] = lax.fori_loop(
            1, n_chan, add, own_part[piece]).astype(jnp.bfloat16)

    @pl.loop(1, n_ctx)
    def _(step):
        peer = lax.rem(me + step, n_ctx)
        out_copy(peer).wait_send()
        back_out(peer).wait_send()

    @pl.loop(1, n_chan)
    def _(step):
        chan = lax.rem(my_chan + step, n_chan)

        @pl.loop(0, chunks)
        def _(piece):
            part_out(chan, piece).wait_send()


def shards(n_ctx, n_chan, query_act, key_act, value_act, filters, skip_scale, w_out):
    block, width = key_act.shape
    feats = w_out.shape[1] // n_chan
    chans = width // n_ctx
    chunk = min(512, feats)
    chunks = feats // chunk
    forward, inverse = tables(block)
    vmem = pl.BlockSpec(memory_space=pltpu.VMEM)
    dma = pltpu.SemaphoreType.DMA
    return pl.pallas_call(
        functools.partial(kernel, n_ctx, n_chan, chunk),
        out_shape=jax.ShapeDtypeStruct((block, feats), jnp.bfloat16),
        in_specs=[vmem] * 7 + [pl.BlockSpec(memory_space=pl.ANY)],
        out_specs=vmem,
        scratch_shapes=[
            pltpu.VMEM((n_ctx, 2 * chans, block), jnp.bfloat16),
            pltpu.VMEM((n_ctx, 2 * chans, block), jnp.bfloat16),
            pltpu.VMEM((n_ctx, 2 * chans // TILE, TILE, 2 * block), jnp.float32),
            pltpu.VMEM((n_ctx, chans // TILE, TILE, 2 * block), jnp.float32),
            pltpu.VMEM((n_ctx, chans, block), jnp.bfloat16),
            pltpu.VMEM((n_ctx, chans, block), jnp.bfloat16),
            pltpu.VMEM(w_out.shape, jnp.bfloat16),
            pltpu.VMEM((n_chan, chunks, block, chunk), jnp.bfloat16),
            pltpu.VMEM((n_chan, chunks, block, chunk), jnp.bfloat16),
            pltpu.VMEM((chunks, block, chunk), jnp.float32),
            dma((n_ctx,)), dma((n_ctx,)), dma((n_ctx,)), dma((n_ctx,)),
            dma((n_chan, chunks)), dma((n_chan, chunks)), dma,
        ],
        compiler_params=pltpu.CompilerParams(
            collective_id=0, has_side_effects=True, vmem_limit_bytes=40 * 1024 * 1024),
    )(query_act, key_act, value_act, filters, skip_scale.reshape(1, width), forward, inverse, w_out)


def solution(mesh):
    return jax.shard_map(
        functools.partial(shards, mesh.shape["ctx"], mesh.shape["chan"]),
        mesh=mesh,
        in_specs=(
            P("ctx", "chan"),
            P("ctx", "chan"),
            P("ctx", "chan"),
            P("ctx", "chan"),
            P("chan"),
            P("chan", None),
        ),
        out_specs=P("ctx", "chan"),
        check_vma=False,
    )
```

time: 181 us -> 43.6 us (0.24)
  waiting for transfers between devices: 75 us -> 0 us
  blocking collectives: 46.6 us -> 0 us
  Pallas kernels: 0 us -> 34.3 us
  starting transfers between devices: 21.6 us -> 0 us
  matrix products: 17.9 us -> 0 us
  between operations: 13.7 us -> 0.02 us
  local copies, waits for them, and re-layouts: 1.78 us -> 9.02 us
  other arithmetic: 4.15 us -> 0 us
    all_to_all x4 -> x0, waiting for transfers between devices: 56.2 us -> none  [the longest x1 21.2 us: shards(): lax.all_to_all(first_section(sent_filter), 'ctx', split_axis=1, concat_ax...]
    all_to_all x2 -> x0, blocking collectives: 46.6 us -> none  [the longest x1 31.8 us: shards(): lax.all_to_all(turned, 'ctx', split_axis=2, concat_axis=1, tiled=True)]
    pallas_call x0 -> x1, Pallas kernels: none -> 34.3 us  [shards(): pl.pallas_call(functools.partial(kernel, n_ctx, n_chan, chunk), out_shape...]
    all_to_all x4 -> x0, starting transfers between devices: 21.3 us -> none  [the longest x1 7.36 us: shards(): lax.all_to_all(gated_in.reshape(1, ctx_size, per_dev, chan_width), 'ctx',...]
    reduce_scatter x1 -> x0, waiting for transfers between devices: 18.8 us -> none  [shards(): lax.psum_scatter(lax.dot_general(w_out, gated, (((0,), (1,)), ((), ())),...]
    dot_general x19 -> x0, matrix products: 17.9 us -> none  [the longest x12 12.8 us: cycle_apply(): return jnp.einsum('kn,zmnc->zmkc', table, operand, precision=precise)]
    unnamed x10 -> x17, local copies, waits for them, and re-layouts: 0.03 us -> 9.02 us
    another operation x3 -> x0, other arithmetic: 2.26 us -> none  [the longest x2 2.19 us: first_section(): jnp.stack([out_real, out_imag]).reshape(2, ctx_size, 2, per_dev, chan_width)]
  transfers between devices with their start and end apart: 5 -> 0, of which waited for: 5 -> 0; matrix products, arithmetic and copies ran while one was open for 3% -> 0% of each run, Pallas kernels for 0% -> 0%
where the time goes in v1:
time: 43.6 us; the launch traced here: 43.3 us
  Pallas kernels  34.3 us (79%)
  local copies, waits for them, and re-layouts  9.02 us (21%)
    pallas_call x1, Pallas kernels, shards(): pl.pallas_call(functools.partial(kernel, n_ctx, n_chan, chunk), out_shape...  34.3 us
    unnamed x17, local copies, waits for them, and re-layouts  9.02 us

profile of v1, /device:TPU:0, one launch (start us, length us, event | category | flops | bytes accessed | tf_op | source)
XLA Modules:
  0.0 43.3 jit_solution(9857815068817063463)
XLA Ops:
  0.0 0.0 copy-start
  0.0 2.2 %copy-done = bf16[512,4096]{1,0:T(8,128)(2,1)S(1)} copy-done((bf16[512,4096]{1,0:T(8,128)(2,1)S(1)}, bf16[512,4096]{1,0:T(8,128)(2,1)}, u32[]{:S(2)}) %copy-start) | copy-done | bytes 4194328
  2.2 0.0 copy-start.1
  2.2 0.9 %copy-done.1 = bf16[128,512]{1,0:T(8,128)(2,1)S(1)} copy-done((bf16[128,512]{1,0:T(8,128)(2,1)S(1)}, bf16[128,512]{1,0:T(8,128)(2,1)}, u32[]{:S(2)}) %copy-start.1) | copy-done | bytes 131096
  3.1 0.0 copy-start.2
  3.1 0.9 %copy-done.2 = bf16[128,512]{1,0:T(8,128)(2,1)S(1)} copy-done((bf16[128,512]{1,0:T(8,128)(2,1)S(1)}, bf16[128,512]{1,0:T(8,128)(2,1)}, u32[]{:S(2)}) %copy-start.2) | copy-done | bytes 131096
  4.0 0.0 copy-start.3
  4.0 0.9 %copy-done.3 = bf16[128,512]{1,0:T(8,128)(2,1)S(1)} copy-done((bf16[128,512]{1,0:T(8,128)(2,1)S(1)}, bf16[128,512]{1,0:T(8,128)(2,1)}, u32[]{:S(2)}) %copy-start.3) | copy-done | bytes 131096
  4.9 0.0 copy-start.4
  4.9 0.9 %copy-done.4 = bf16[128,512]{1,0:T(8,128)(2,1)S(1)} copy-done((bf16[128,512]{1,0:T(8,128)(2,1)S(1)}, bf16[128,512]{1,0:T(8,128)(2,1)}, u32[]{:S(2)}) %copy-start.4) | copy-done | bytes 131096
  5.8 0.0 copy-start.5
  5.8 0.9 %copy-done.5 = bf16[256,256]{1,0:T(8,128)(2,1)S(1)} copy-done((bf16[256,256]{1,0:T(8,128)(2,1)S(1)}, bf16[256,256]{1,0:T(8,128)(2,1)}, u32[]{:S(2)}) %copy-start.5) | copy-done | bytes 131096
  6.7 0.0 copy-start.6
  6.7 0.8 %copy-done.6 = bf16[128,256]{1,0:T(8,128)(2,1)S(1)} copy-done((bf16[128,256]{1,0:T(8,128)(2,1)S(1)}, bf16[128,256]{1,0:T(8,128)(2,1)}, u32[]{:S(2)}) %copy-start.6) | copy-done | bytes 65560
  7.6 0.0 copy-start.7
  7.6 0.7 %copy-done.7 = f32[512]{0:T(512)S(1)} copy-done((f32[512]{0:T(512)S(1)}, f32[512]{0:T(512)}, u32[]{:S(2)}) %copy-start.7) | copy-done | bytes 2072
  8.2 34.3 %shard_map.82 = bf16[128,2048]{1,0:T(8,128)(2,1)S(1)} custom-call(bf16[128,512]{1,0:T(8,128)(2,1)S(1)} %copy-done.1, bf16[128,512]{1,0:T(8,128)(2,1)S(1)} %copy-done.2, bf16[128,512]{1,0:T(8,128)(2,1)S(1)} %copy-done.3, bf16[128,512]{1,0:T(8,128)(2,1)S(1)} %copy-done.4, f32[1,512]{1,0:T(1,128)S(1)} %bitcast.1, bf16[128,256]{1,0:T(8,128)(2,1)S(1)} %copy-done.6, ...), custom_call_target="tpu_custom_call" | custom-call | tf_op jit(solution)/shard_map/pallas_call | solution.py:208
  42.5 0.8 %copy.10 = bf16[128,2048]{1,0:T(8,128)(2,1)} copy(bf16[128,2048]{1,0:T(8,128)(2,1)S(1)} %shard_map.82) | data formatting | bytes 1048576
Async XLA Ops:
  0.0 2.2 %copy-start = (bf16[512,4096]{1,0:T(8,128)(2,1)S(1)}, bf16[512,4096]{1,0:T(8,128)(2,1)}, u32[]{:S(2)}) copy-start(bf16[512,4096]{1,0:T(8,128)(2,1)} %w_ref.1) | copy-start | bytes 12582916
  2.2 0.9 %copy-start.1 = (bf16[128,512]{1,0:T(8,128)(2,1)S(1)}, bf16[128,512]{1,0:T(8,128)(2,1)}, u32[]{:S(2)}) copy-start(bf16[128,512]{1,0:T(8,128)(2,1)} %query_ref.1) | copy-start | bytes 393220
  3.1 0.9 %copy-start.2 = (bf16[128,512]{1,0:T(8,128)(2,1)S(1)}, bf16[128,512]{1,0:T(8,128)(2,1)}, u32[]{:S(2)}) copy-start(bf16[128,512]{1,0:T(8,128)(2,1)} %key_ref.1) | copy-start | bytes 393220
  4.0 0.9 %copy-start.3 = (bf16[128,512]{1,0:T(8,128)(2,1)S(1)}, bf16[128,512]{1,0:T(8,128)(2,1)}, u32[]{:S(2)}) copy-start(bf16[128,512]{1,0:T(8,128)(2,1)} %value_ref.1) | copy-start | bytes 393220
  4.9 0.9 %copy-start.4 = (bf16[128,512]{1,0:T(8,128)(2,1)S(1)}, bf16[128,512]{1,0:T(8,128)(2,1)}, u32[]{:S(2)}) copy-start(bf16[128,512]{1,0:T(8,128)(2,1)} %filter_ref.1) | copy-start | bytes 393220
  5.8 0.9 %copy-start.5 = (bf16[256,256]{1,0:T(8,128)(2,1)S(1)}, bf16[256,256]{1,0:T(8,128)(2,1)}, u32[]{:S(2)}) copy-start(bf16[256,256]{1,0:T(8,128)(2,1)} %constant.5.clone.inv_ref) | copy-start | bytes 393220
  6.7 0.8 %copy-start.6 = (bf16[128,256]{1,0:T(8,128)(2,1)S(1)}, bf16[128,256]{1,0:T(8,128)(2,1)}, u32[]{:S(2)}) copy-start(bf16[128,256]{1,0:T(8,128)(2,1)} %constant.4.clone.fwd_ref) | copy-start | bytes 196612
  7.6 0.7 %copy-start.7 = (f32[512]{0:T(512)S(1)}, f32[512]{0:T(512)}, u32[]{:S(2)}) copy-start(f32[512]{0:T(512)} %param.12) | copy-start | bytes 6148

commit v2 on v1

--- a/solution.py
+++ b/solution.py
@@ -11,6 +11,9 @@
 
 MESH = pl.DeviceIdType.MESH
 TILE = 8
+LANES = 128
+PIECES = 4
+AHEAD = 3
 
 
 def tables(block):
@@ -23,19 +26,68 @@
 
 
 def kernel(
-    n_ctx, n_chan, chunk,
-    query_ref, key_ref, value_ref, filter_ref, skip_ref, fwd_ref, inv_ref, w_ref,
+    n_ctx, n_chan,
+    query_hbm, key_hbm, value_hbm, filter_hbm, skip_hbm, fwd_hbm, inv_hbm, w_ref,
     out_ref,
-    send, recv, spec, prod, back_send, back_recv, w_vmem, part_send, part_recv, own_part,
-    send_sem, recv_sem, back_send_sem, back_recv_sem, part_send_sem, part_recv_sem, w_sem,
+    query_ref, key_ref, value_ref, filter_ref, skip_ref, fwd_ref, inv_ref,
+    send, recv, spec, prod, back_send, back_recv, w_vmem, w_other, gated, gated_recv, part_send, part_recv, own_part,
+    send_sem, recv_sem, back_send_sem, back_recv_sem, part_send_sem, part_recv_sem, load_sem,
+    w_send_sem, w_recv_sem, pair_send_sem, pair_recv_sem, gated_send_sem, gated_recv_sem,
 ):
     me = lax.axis_index("ctx")
     my_chan = lax.axis_index("chan")
     block, width = key_ref.shape
+    loads = [
+        pltpu.make_async_copy(source, target, load_sem.at[i])
+        for i, (source, target) in enumerate([
+            (key_hbm, key_ref), (value_hbm, value_ref), (filter_hbm, filter_ref), (fwd_hbm, fwd_ref),
+            (inv_hbm, inv_ref), (query_hbm, query_ref), (skip_hbm, skip_ref), (w_ref, w_vmem)])
+    ]
+    for load in loads:
+        load.start()
     chans = width // n_ctx
     groups = chans // TILE
     feats = out_ref.shape[1]
-    chunks = feats // chunk
+    chunk = feats // PIECES
+    ahead = AHEAD * chunk
+    core = lax.rem(me, 2)
+    sibling = me + 1 - 2 * core
+    w_rows = width // 2 // PIECES
+
+    def other(step):
+        return lax.rem(my_chan + step, n_chan)
+
+    def row_range(half, piece):
+        return pl.ds(pl.multiple_of(half * (width // 2) + piece * w_rows, w_rows), w_rows)
+
+    def w_move(chan, source, piece):
+        rows = row_range(core, piece)
+        return pltpu.make_async_remote_copy(
+            src_ref=w_ref.at[rows, pl.ds(pl.multiple_of(chan * feats, chunk), ahead)],
+            dst_ref=w_other.at[source, rows, :],
+            send_sem=w_send_sem.at[chan, piece], recv_sem=w_recv_sem.at[source, piece],
+            device_id={"chan": chan}, device_id_type=MESH)
+
+    def pair_move(chan, half, piece):
+        rows = row_range(half, piece)
+        return pltpu.make_async_remote_copy(
+            src_ref=w_other.at[chan, rows, :], dst_ref=w_other.at[chan, rows, :],
+            send_sem=pair_send_sem.at[chan, piece], recv_sem=pair_recv_sem.at[chan, piece],
+            device_id={"ctx": sibling}, device_id_type=MESH)
+
+    def hand_over(piece):
+        @pl.loop(1, n_chan)
+        def _(step):
+            chan = other(step)
+            w_move(chan, chan, piece).wait_recv()
+            pair_move(chan, core, piece).start()
+
+    def gated_move(chan, source, piece):
+        columns = pl.ds(piece * LANES, LANES)
+        return pltpu.make_async_remote_copy(
+            src_ref=gated.at[:, columns], dst_ref=gated_recv.at[source, :, columns],
+            send_sem=gated_send_sem.at[chan, piece], recv_sem=gated_recv_sem.at[source, piece],
+            device_id={"chan": chan}, device_id_type=MESH)
 
     barrier = pltpu.get_barrier_semaphore()
 
@@ -47,9 +99,8 @@
     def _(step):
         pl.semaphore_signal(barrier, inc=1, device_id={"chan": lax.rem(my_chan + step, n_chan)}, device_id_type=MESH)
 
-    w_copy = pltpu.make_async_copy(w_ref, w_vmem, w_sem)
-    w_copy.start()
-
+    for load in loads[:3]:
+        load.wait()
     gated_in = (key_ref[...].astype(jnp.float32) * value_ref[...].astype(jnp.float32)).astype(jnp.bfloat16).astype(jnp.float32)
     signal_t = gated_in.T.reshape(n_ctx, chans, block)
     filter_t = filter_ref[...].astype(jnp.float32).T.reshape(n_ctx, chans, block)
@@ -73,12 +124,21 @@
     def _(step):
         out_copy(lax.rem(me + step, n_ctx)).start()
 
+    @pl.loop(1, n_chan)
+    def _(step):
+        chan = other(step)
+
+        @pl.loop(0, PIECES)
+        def _(piece):
+            w_move(chan, my_chan, piece).start()
+
     recv[me] = send[me]
 
     @pl.loop(1, n_ctx)
     def _(step):
         in_copy(lax.rem(me + step, n_ctx)).wait_recv()
 
+    loads[3].wait()
     spec[...] = jnp.dot(
         recv[...].reshape(n_ctx * 2 * chans, block), fwd_ref[...], preferred_element_type=jnp.float32
     ).reshape(n_ctx, 2 * groups, TILE, 2 * block)
@@ -110,6 +170,8 @@
                 prod[tile * TILE + i, group, :, low] = acc[2 * i]
                 prod[tile * TILE + i, group, :, high] = acc[2 * i + 1]
 
+    hand_over(0)
+    loads[4].wait()
     mixed = jnp.dot(
         prod[...].reshape(n_ctx * chans, 2 * block).astype(jnp.bfloat16), inv_ref[...],
         preferred_element_type=jnp.float32)
@@ -134,52 +196,75 @@
         back_out(lax.rem(me + step, n_ctx)).start()
 
     back_recv[me] = back_send[me]
-    w_copy.wait()
-
-    @pl.loop(1, n_ctx)
-    def _(step):
-        back_in(lax.rem(me + step, n_ctx)).wait_recv()
-
-    convolved = back_recv[...].astype(jnp.float32).reshape(width, block).T
-    signal = (key_ref[...].astype(jnp.float32) * value_ref[...].astype(jnp.float32)).astype(jnp.bfloat16).astype(jnp.float32)
-    gated = (query_ref[...].astype(jnp.float32) * (convolved + skip_ref[...] * signal)).astype(jnp.bfloat16)
+    for load in loads[5:]:
+        load.wait()
+    hand_over(1)
+
+    lots = width // LANES
+    peers = n_ctx // lots
+    for lot in range(lots):
+        for peer in range(lot * peers, (lot + 1) * peers):
+            @pl.when(peer != me)
+            def _():
+                back_in(peer).wait_recv()
+        lanes = slice(lot * LANES, (lot + 1) * LANES)
+        convolved = back_recv[lot * peers:(lot + 1) * peers].astype(jnp.float32).reshape(LANES, block).T
+        signal = (key_ref[:, lanes].astype(jnp.float32) * value_ref[:, lanes].astype(jnp.float32)).astype(jnp.bfloat16).astype(jnp.float32)
+        gated[:, lanes] = (
+            query_ref[:, lanes].astype(jnp.float32) * (convolved + skip_ref[:, lanes] * signal)).astype(jnp.bfloat16)
+
+        @pl.loop(1, n_chan)
+        def _(step):
+            gated_move(other(step), my_chan, lot).start()
 
     def product(chan, piece):
         columns = pl.ds(pl.multiple_of(chan * feats + piece * chunk, chunk), chunk)
-        return jnp.dot(gated, w_vmem[:, columns], preferred_element_type=jnp.float32)
-
-    def part_out(chan, piece):
-        return pltpu.make_async_remote_copy(
-            src_ref=part_send.at[chan, piece], dst_ref=part_recv.at[my_chan, piece],
-            send_sem=part_send_sem.at[chan, piece], recv_sem=part_recv_sem.at[my_chan, piece],
+        return jnp.dot(gated[...], w_vmem[:, columns], preferred_element_type=jnp.float32)
+
+    def part_move(chan, source, piece):
+        return pltpu.make_async_remote_copy(
+            src_ref=part_send.at[chan, piece], dst_ref=part_recv.at[source, piece],
+            send_sem=part_send_sem.at[chan, piece], recv_sem=part_recv_sem.at[source, piece],
             device_id={"chan": chan}, device_id_type=MESH)
 
-    def part_in(chan, piece):
-        return pltpu.make_async_remote_copy(
-            src_ref=part_send.at[my_chan, piece], dst_ref=part_recv.at[chan, piece],
-            send_sem=part_send_sem.at[my_chan, piece], recv_sem=part_recv_sem.at[chan, piece],
-            device_id={"chan": chan}, device_id_type=MESH)
-
-    @pl.loop(1, n_chan)
-    def _(step):
-        chan = lax.rem(my_chan + step, n_chan)
-
-        @pl.loop(0, chunks)
-        def _(piece):
-            part_send[chan, piece] = product(chan, piece).astype(jnp.bfloat16)
-            part_out(chan, piece).start()
-
-    @pl.loop(0, chunks)
-    def _(piece):
-        own_part[piece] = product(my_chan, piece).astype(jnp.bfloat16).astype(jnp.float32)
-
-    for piece in range(chunks):
+    @pl.loop(1, n_chan)
+    def _(step):
+        chan = other(step)
+        for piece in range(PIECES - AHEAD):
+            part_send[chan, piece] = product(chan, AHEAD + piece).astype(jnp.bfloat16)
+            part_move(chan, my_chan, piece).start()
+
+    for piece in range(2, PIECES):
+        hand_over(piece)
+
+    for piece in range(PIECES):
+        own_part[piece] = product(my_chan, piece)
+
+    @pl.loop(1, n_chan)
+    def _(step):
+        chan = other(step)
+        for piece in range(PIECES):
+            pair_move(chan, 1 - core, piece).wait_recv()
+        for lot in range(lots):
+            gated_move(chan, chan, lot).wait_recv()
+
+    for piece in range(AHEAD):
+        columns = slice(piece * chunk, (piece + 1) * chunk)
+
+        def gather(step, total):
+            chan = other(step)
+            return total + jnp.dot(
+                gated_recv[chan], w_other[chan, :, columns], preferred_element_type=jnp.float32)
+        out_ref[:, columns] = lax.fori_loop(1, n_chan, gather, own_part[piece]).astype(jnp.bfloat16)
+
+    for piece in range(PIECES - AHEAD):
+        columns = slice((AHEAD + piece) * chunk, (AHEAD + piece + 1) * chunk)
+
         def add(step, total):
-            chan = lax.rem(my_chan + step, n_chan)
-            part_in(chan, piece).wait_recv()
+            chan = other(step)
+            part_move(chan, chan, piece).wait_recv()
             return total + part_recv[chan, piece].astype(jnp.float32)
-        out_ref[:, piece * chunk:(piece + 1) * chunk] = lax.fori_loop(
-            1, n_chan, add, own_part[piece]).astype(jnp.bfloat16)
+        out_ref[:, columns] = lax.fori_loop(1, n_chan, add, own_part[AHEAD + piece]).astype(jnp.bfloat16)
 
     @pl.loop(1, n_ctx)
     def _(step):
@@ -189,28 +274,35 @@
 
     @pl.loop(1, n_chan)
     def _(step):
-        chan = lax.rem(my_chan + step, n_chan)
-
-        @pl.loop(0, chunks)
-        def _(piece):
-            part_out(chan, piece).wait_send()
+        chan = other(step)
+        for piece in range(PIECES):
+            w_move(chan, my_chan, piece).wait_send()
+            pair_move(chan, core, piece).wait_send()
+        for lot in range(lots):
+            gated_move(chan, my_chan, lot).wait_send()
+        for piece in range(PIECES - AHEAD):
+            part_move(chan, my_chan, piece).wait_send()
 
 
 def shards(n_ctx, n_chan, query_act, key_act, value_act, filters, skip_scale, w_out):
     block, width = key_act.shape
     feats = w_out.shape[1] // n_chan
     chans = width // n_ctx
-    chunk = min(512, feats)
-    chunks = feats // chunk
+    chunk = feats // PIECES
+    rest = PIECES - AHEAD
+    lots = width // LANES
     forward, inverse = tables(block)
     vmem = pl.BlockSpec(memory_space=pltpu.VMEM)
     dma = pltpu.SemaphoreType.DMA
     return pl.pallas_call(
-        functools.partial(kernel, n_ctx, n_chan, chunk),
+        functools.partial(kernel, n_ctx, n_chan),
         out_shape=jax.ShapeDtypeStruct((block, feats), jnp.bfloat16),
-        in_specs=[vmem] * 7 + [pl.BlockSpec(memory_space=pl.ANY)],
+        in_specs=[pl.BlockSpec(memory_space=pltpu.HBM)] * 8,
         out_specs=vmem,
-        scratch_shapes=[
+        scratch_shapes=[pltpu.VMEM((block, width), jnp.bfloat16)] * 4 + [
+            pltpu.VMEM((1, width), jnp.float32),
+            pltpu.VMEM(forward.shape, jnp.bfloat16),
+            pltpu.VMEM(inverse.shape, jnp.bfloat16),
             pltpu.VMEM((n_ctx, 2 * chans, block), jnp.bfloat16),
             pltpu.VMEM((n_ctx, 2 * chans, block), jnp.bfloat16),
             pltpu.VMEM((n_ctx, 2 * chans // TILE, TILE, 2 * block), jnp.float32),
@@ -218,14 +310,19 @@
             pltpu.VMEM((n_ctx, chans, block), jnp.bfloat16),
             pltpu.VMEM((n_ctx, chans, block), jnp.bfloat16),
             pltpu.VMEM(w_out.shape, jnp.bfloat16),
-            pltpu.VMEM((n_chan, chunks, block, chunk), jnp.bfloat16),
-            pltpu.VMEM((n_chan, chunks, block, chunk), jnp.bfloat16),
-            pltpu.VMEM((chunks, block, chunk), jnp.float32),
+            pltpu.VMEM((n_chan, width, AHEAD * chunk), jnp.bfloat16),
+            pltpu.VMEM((block, width), jnp.bfloat16),
+            pltpu.VMEM((n_chan, block, width), jnp.bfloat16),
+            pltpu.VMEM((n_chan, rest, block, chunk), jnp.bfloat16),
+            pltpu.VMEM((n_chan, rest, block, chunk), jnp.bfloat16),
+            pltpu.VMEM((PIECES, block, chunk), jnp.float32),
             dma((n_ctx,)), dma((n_ctx,)), dma((n_ctx,)), dma((n_ctx,)),
-            dma((n_chan, chunks)), dma((n_chan, chunks)), dma,
+            dma((n_chan, rest)), dma((n_chan, rest)), dma((8,)),
+            dma((n_chan, PIECES)), dma((n_chan, PIECES)), dma((n_chan, PIECES)), dma((n_chan, PIECES)),
+            dma((n_chan, lots)), dma((n_chan, lots)),
         ],
         compiler_params=pltpu.CompilerParams(
-            collective_id=0, has_side_effects=True, vmem_limit_bytes=40 * 1024 * 1024),
+            collective_id=0, has_side_effects=True, vmem_limit_bytes=62 * 1024 * 1024),
     )(query_act, key_act, value_act, filters, skip_scale.reshape(1, width), forward, inverse, w_out)
 
 

time: 43.6 us -> 35.3 us (0.81)
  local copies, waits for them, and re-layouts: 9.02 us -> 1.88 us
  Pallas kernels: 34.3 us -> 33.3 us
    unnamed x17 -> x1, local copies, waits for them, and re-layouts: 9.02 us -> 1.88 us
    pallas_call x1, Pallas kernels: 34.3 us -> 33.3 us  [shards(): pl.pallas_call(functools.partial(kernel, n_ctx, n_chan), out_shape=jax.Sh...]
where the time goes in v2:
time: 35.3 us; the launch traced here: 35.2 us
  Pallas kernels  33.3 us (94%)
  local copies, waits for them, and re-layouts  1.88 us (5%)
    pallas_call x1, Pallas kernels, shards(): pl.pallas_call(functools.partial(kernel, n_ctx, n_chan), out_shape=jax.Sh...  33.3 us
    unnamed x1, local copies, waits for them, and re-layouts  1.88 us

profile of v2, /device:TPU:0, one launch (start us, length us, event | category | flops | bytes accessed | tf_op | source)
XLA Modules:
  0.0 35.2 jit_solution(2265544159177565096)
XLA Ops:
  0.0 33.3 %shard_map.82 = bf16[128,2048]{1,0:T(8,128)(2,1)} custom-call(bf16[128,512]{1,0:T(8,128)(2,1)} %query_hbm.1, bf16[128,512]{1,0:T(8,128)(2,1)} %key_hbm.1, bf16[128,512]{1,0:T(8,128)(2,1)} %value_hbm.1, bf16[128,512]{1,0:T(8,128)(2,1)} %filter_hbm.1, f32[1,512]{1,0:T(1,128)} %bitcast.1, bf16[128,256]{1,0:T(8,128)(2,1)} %constant.4.clone.fwd_hbm, ...), custom_call_target="tpu_custom_call" | custom-call | tf_op jit(solution)/shard_map/pallas_call | solution.py:297
  33.3 1.9 %copy.10 = bf16[128,2048]{1,0:T(8,128)(2,1)} copy(bf16[128,2048]{1,0:T(8,128)(2,1)} %shard_map.82) | data formatting | bytes 1048576

commit v3 on v2

--- a/solution.py
+++ b/solution.py
@@ -13,7 +13,8 @@
 TILE = 8
 LANES = 128
 PIECES = 4
-AHEAD = 3
+AHEAD = 4
+W_PIECES = 4
 
 
 def tables(block):
@@ -32,7 +33,7 @@
     query_ref, key_ref, value_ref, filter_ref, skip_ref, fwd_ref, inv_ref,
     send, recv, spec, prod, back_send, back_recv, w_vmem, w_other, gated, gated_recv, part_send, part_recv, own_part,
     send_sem, recv_sem, back_send_sem, back_recv_sem, part_send_sem, part_recv_sem, load_sem,
-    w_send_sem, w_recv_sem, pair_send_sem, pair_recv_sem, gated_send_sem, gated_recv_sem,
+    w_send_sem, w_recv_sem, side_send_sem, side_recv_sem, pair_send_sem, pair_recv_sem, gated_send_sem, gated_recv_sem,
 ):
     me = lax.axis_index("ctx")
     my_chan = lax.axis_index("chan")
@@ -50,29 +51,37 @@
     feats = out_ref.shape[1]
     chunk = feats // PIECES
     ahead = AHEAD * chunk
-    core = lax.rem(me, 2)
-    sibling = me + 1 - 2 * core
-    w_rows = width // 2 // PIECES
+    core, side = lax.rem(me, 2), lax.rem(me // 2, 2)
+    sibling, across = me + 1 - 2 * core, me + 2 - 4 * side
+    quarter, far_quarter = 2 * side + core, 2 - 2 * side + core
+    w_rows = width // 4 // W_PIECES
 
     def other(step):
         return lax.rem(my_chan + step, n_chan)
 
-    def row_range(half, piece):
-        return pl.ds(pl.multiple_of(half * (width // 2) + piece * w_rows, w_rows), w_rows)
+    def row_range(part, piece):
+        return pl.ds(pl.multiple_of(part * (width // 4) + piece * w_rows, w_rows), w_rows)
 
     def w_move(chan, source, piece):
-        rows = row_range(core, piece)
+        rows = row_range(quarter, piece)
         return pltpu.make_async_remote_copy(
             src_ref=w_ref.at[rows, pl.ds(pl.multiple_of(chan * feats, chunk), ahead)],
             dst_ref=w_other.at[source, rows, :],
             send_sem=w_send_sem.at[chan, piece], recv_sem=w_recv_sem.at[source, piece],
             device_id={"chan": chan}, device_id_type=MESH)
 
-    def pair_move(chan, half, piece):
-        rows = row_range(half, piece)
+    def side_move(chan, part, piece):
+        rows = row_range(part, piece)
         return pltpu.make_async_remote_copy(
             src_ref=w_other.at[chan, rows, :], dst_ref=w_other.at[chan, rows, :],
-            send_sem=pair_send_sem.at[chan, piece], recv_sem=pair_recv_sem.at[chan, piece],
+            send_sem=side_send_sem.at[chan, piece], recv_sem=side_recv_sem.at[chan, piece],
+            device_id={"ctx": across}, device_id_type=MESH)
+
+    def pair_move(chan, part, piece, origin):
+        rows = row_range(part, piece)
+        return pltpu.make_async_remote_copy(
+            src_ref=w_other.at[chan, rows, :], dst_ref=w_other.at[chan, rows, :],
+            send_sem=pair_send_sem.at[chan, origin, piece], recv_sem=pair_recv_sem.at[chan, origin, piece],
             device_id={"ctx": sibling}, device_id_type=MESH)
 
     def hand_over(piece):
@@ -80,7 +89,15 @@
         def _(step):
             chan = other(step)
             w_move(chan, chan, piece).wait_recv()
-            pair_move(chan, core, piece).start()
+            side_move(chan, quarter, piece).start()
+            pair_move(chan, quarter, piece, 0).start()
+
+    def hand_on(piece):
+        @pl.loop(1, n_chan)
+        def _(step):
+            chan = other(step)
+            side_move(chan, far_quarter, piece).wait_recv()
+            pair_move(chan, far_quarter, piece, 1).start()
 
     def gated_move(chan, source, piece):
         columns = pl.ds(piece * LANES, LANES)
@@ -128,16 +145,18 @@
     def _(step):
         chan = other(step)
 
-        @pl.loop(0, PIECES)
+        @pl.loop(0, W_PIECES)
         def _(piece):
             w_move(chan, my_chan, piece).start()
 
     recv[me] = send[me]
+    hand_over(0)
 
     @pl.loop(1, n_ctx)
     def _(step):
         in_copy(lax.rem(me + step, n_ctx)).wait_recv()
 
+    hand_over(1)
     loads[3].wait()
     spec[...] = jnp.dot(
         recv[...].reshape(n_ctx * 2 * chans, block), fwd_ref[...], preferred_element_type=jnp.float32
@@ -170,7 +189,6 @@
                 prod[tile * TILE + i, group, :, low] = acc[2 * i]
                 prod[tile * TILE + i, group, :, high] = acc[2 * i + 1]
 
-    hand_over(0)
     loads[4].wait()
     mixed = jnp.dot(
         prod[...].reshape(n_ctx * chans, 2 * block).astype(jnp.bfloat16), inv_ref[...],
@@ -198,7 +216,10 @@
     back_recv[me] = back_send[me]
     for load in loads[5:]:
         load.wait()
-    hand_over(1)
+    for piece in range(2, W_PIECES):
+        hand_over(piece)
+    for piece in range(W_PIECES - 1):
+        hand_on(piece)
 
     lots = width // LANES
     peers = n_ctx // lots
@@ -234,8 +255,7 @@
             part_send[chan, piece] = product(chan, AHEAD + piece).astype(jnp.bfloat16)
             part_move(chan, my_chan, piece).start()
 
-    for piece in range(2, PIECES):
-        hand_over(piece)
+    hand_on(W_PIECES - 1)
 
     for piece in range(PIECES):
         own_part[piece] = product(my_chan, piece)
@@ -243,8 +263,9 @@
     @pl.loop(1, n_chan)
     def _(step):
         chan = other(step)
-        for piece in range(PIECES):
-            pair_move(chan, 1 - core, piece).wait_recv()
+        for piece in range(W_PIECES):
+            pair_move(chan, 2 * side + 1 - core, piece, 0).wait_recv()
+            pair_move(chan, 3 - 2 * side - core, piece, 1).wait_recv()
         for lot in range(lots):
             gated_move(chan, chan, lot).wait_recv()
 
@@ -275,9 +296,11 @@
     @pl.loop(1, n_chan)
     def _(step):
         chan = other(step)
-        for piece in range(PIECES):
+        for piece in range(W_PIECES):
             w_move(chan, my_chan, piece).wait_send()
-            pair_move(chan, core, piece).wait_send()
+            side_move(chan, quarter, piece).wait_send()
+            pair_move(chan, quarter, piece, 0).wait_send()
+            pair_move(chan, far_quarter, piece, 1).wait_send()
         for lot in range(lots):
             gated_move(chan, my_chan, lot).wait_send()
         for piece in range(PIECES - AHEAD):
@@ -289,7 +312,7 @@
     feats = w_out.shape[1] // n_chan
     chans = width // n_ctx
     chunk = feats // PIECES
-    rest = PIECES - AHEAD
+    rest = max(PIECES - AHEAD, 1)
     lots = width // LANES
     forward, inverse = tables(block)
     vmem = pl.BlockSpec(memory_space=pltpu.VMEM)
@@ -318,7 +341,8 @@
             pltpu.VMEM((PIECES, block, chunk), jnp.float32),
             dma((n_ctx,)), dma((n_ctx,)), dma((n_ctx,)), dma((n_ctx,)),
             dma((n_chan, rest)), dma((n_chan, rest)), dma((8,)),
-            dma((n_chan, PIECES)), dma((n_chan, PIECES)), dma((n_chan, PIECES)), dma((n_chan, PIECES)),
+            dma((n_chan, W_PIECES)), dma((n_chan, W_PIECES)), dma((n_chan, W_PIECES)), dma((n_chan, W_PIECES)),
+            dma((n_chan, 2, W_PIECES)), dma((n_chan, 2, W_PIECES)),
             dma((n_chan, lots)), dma((n_chan, lots)),
         ],
         compiler_params=pltpu.CompilerParams(

time: 35.3 us -> 31.7 us (0.90)
  Pallas kernels: 33.3 us -> 29.6 us
    pallas_call x1, Pallas kernels: 33.3 us -> 29.6 us  [shards(): pl.pallas_call(functools.partial(kernel, n_ctx, n_chan), out_shape=jax.Sh...]
where the time goes in v3:
time: 31.7 us; the launch traced here: 31.5 us
  Pallas kernels  29.6 us (93%)
  local copies, waits for them, and re-layouts  1.88 us (6%)
    pallas_call x1, Pallas kernels, shards(): pl.pallas_call(functools.partial(kernel, n_ctx, n_chan), out_shape=jax.Sh...  29.6 us
    unnamed x1, local copies, waits for them, and re-layouts  1.88 us

profile of v3, /device:TPU:0, one launch (start us, length us, event | category | flops | bytes accessed | tf_op | source)
XLA Modules:
  0.0 31.5 jit_solution(5287142159565940403)
XLA Ops:
  0.0 29.6 %shard_map.82 = bf16[128,2048]{1,0:T(8,128)(2,1)} custom-call(bf16[128,512]{1,0:T(8,128)(2,1)} %query_hbm.1, bf16[128,512]{1,0:T(8,128)(2,1)} %key_hbm.1, bf16[128,512]{1,0:T(8,128)(2,1)} %value_hbm.1, bf16[128,512]{1,0:T(8,128)(2,1)} %filter_hbm.1, f32[1,512]{1,0:T(1,128)} %bitcast.1, bf16[128,256]{1,0:T(8,128)(2,1)} %constant.4.clone.fwd_hbm, ...), custom_call_target="tpu_custom_call" | custom-call | tf_op jit(solution)/shard_map/pallas_call | solution.py:320
  29.6 1.9 %copy.10 = bf16[128,2048]{1,0:T(8,128)(2,1)} copy(bf16[128,2048]{1,0:T(8,128)(2,1)} %shard_map.82) | data formatting | bytes 1048576

commit v4 on v3

--- a/solution.py
+++ b/solution.py
@@ -33,7 +33,7 @@
     query_ref, key_ref, value_ref, filter_ref, skip_ref, fwd_ref, inv_ref,
     send, recv, spec, prod, back_send, back_recv, w_vmem, w_other, gated, gated_recv, part_send, part_recv, own_part,
     send_sem, recv_sem, back_send_sem, back_recv_sem, part_send_sem, part_recv_sem, load_sem,
-    w_send_sem, w_recv_sem, side_send_sem, side_recv_sem, pair_send_sem, pair_recv_sem, gated_send_sem, gated_recv_sem,
+    w_send_sem, w_recv_sem, side_send_sem, side_recv_sem, pair_send_sem, pair_recv_sem, gated_send_sem, gated_recv_sem, out_vmem, out_sem,
 ):
     me = lax.axis_index("ctx")
     my_chan = lax.axis_index("chan")
@@ -137,10 +137,6 @@
             send_sem=send_sem.at[me], recv_sem=recv_sem.at[peer],
             device_id={"ctx": peer}, device_id_type=MESH)
 
-    @pl.loop(1, n_ctx)
-    def _(step):
-        out_copy(lax.rem(me + step, n_ctx)).start()
-
     @pl.loop(1, n_chan)
     def _(step):
         chan = other(step)
@@ -148,6 +144,10 @@
         @pl.loop(0, W_PIECES)
         def _(piece):
             w_move(chan, my_chan, piece).start()
+
+    @pl.loop(1, n_ctx)
+    def _(step):
+        out_copy(lax.rem(me + step, n_ctx)).start()
 
     recv[me] = send[me]
     hand_over(0)
@@ -218,8 +218,6 @@
         load.wait()
     for piece in range(2, W_PIECES):
         hand_over(piece)
-    for piece in range(W_PIECES - 1):
-        hand_on(piece)
 
     lots = width // LANES
     peers = n_ctx // lots
@@ -255,7 +253,8 @@
             part_send[chan, piece] = product(chan, AHEAD + piece).astype(jnp.bfloat16)
             part_move(chan, my_chan, piece).start()
 
-    hand_on(W_PIECES - 1)
+    for piece in range(W_PIECES):
+        hand_on(piece)
 
     for piece in range(PIECES):
         own_part[piece] = product(my_chan, piece)
@@ -269,6 +268,10 @@
         for lot in range(lots):
             gated_move(chan, chan, lot).wait_recv()
 
+    def out_move(piece):
+        columns = pl.ds(piece * chunk, chunk)
+        return pltpu.make_async_copy(out_vmem.at[:, columns], out_ref.at[:, columns], out_sem.at[piece])
+
     for piece in range(AHEAD):
         columns = slice(piece * chunk, (piece + 1) * chunk)
 
@@ -276,7 +279,8 @@
             chan = other(step)
             return total + jnp.dot(
                 gated_recv[chan], w_other[chan, :, columns], preferred_element_type=jnp.float32)
-        out_ref[:, columns] = lax.fori_loop(1, n_chan, gather, own_part[piece]).astype(jnp.bfloat16)
+        out_vmem[:, columns] = lax.fori_loop(1, n_chan, gather, own_part[piece]).astype(jnp.bfloat16)
+        out_move(piece).start()
 
     for piece in range(PIECES - AHEAD):
         columns = slice((AHEAD + piece) * chunk, (AHEAD + piece + 1) * chunk)
@@ -285,7 +289,8 @@
             chan = other(step)
             part_move(chan, chan, piece).wait_recv()
             return total + part_recv[chan, piece].astype(jnp.float32)
-        out_ref[:, columns] = lax.fori_loop(1, n_chan, add, own_part[AHEAD + piece]).astype(jnp.bfloat16)
+        out_vmem[:, columns] = lax.fori_loop(1, n_chan, add, own_part[AHEAD + piece]).astype(jnp.bfloat16)
+        out_move(AHEAD + piece).start()
 
     @pl.loop(1, n_ctx)
     def _(step):
@@ -305,6 +310,9 @@
             gated_move(chan, my_chan, lot).wait_send()
         for piece in range(PIECES - AHEAD):
             part_move(chan, my_chan, piece).wait_send()
+
+    for piece in range(PIECES):
+        out_move(piece).wait()
 
 
 def shards(n_ctx, n_chan, query_act, key_act, value_act, filters, skip_scale, w_out):
@@ -321,7 +329,7 @@
         functools.partial(kernel, n_ctx, n_chan),
         out_shape=jax.ShapeDtypeStruct((block, feats), jnp.bfloat16),
         in_specs=[pl.BlockSpec(memory_space=pltpu.HBM)] * 8,
-        out_specs=vmem,
+        out_specs=pl.BlockSpec(memory_space=pltpu.HBM),
         scratch_shapes=[pltpu.VMEM((block, width), jnp.bfloat16)] * 4 + [
             pltpu.VMEM((1, width), jnp.float32),
             pltpu.VMEM(forward.shape, jnp.bfloat16),
@@ -344,6 +352,7 @@
             dma((n_chan, W_PIECES)), dma((n_chan, W_PIECES)), dma((n_chan, W_PIECES)), dma((n_chan, W_PIECES)),
             dma((n_chan, 2, W_PIECES)), dma((n_chan, 2, W_PIECES)),
             dma((n_chan, lots)), dma((n_chan, lots)),
+            pltpu.VMEM((block, feats), jnp.bfloat16), dma((PIECES,)),
         ],
         compiler_params=pltpu.CompilerParams(
             collective_id=0, has_side_effects=True, vmem_limit_bytes=62 * 1024 * 1024),

time: 31.7 us -> 30.9 us (0.975)
  the two profiles are of different devices: /device:TPU:0 before, /device:TPU:1 now
where the time goes in v4:
time: 30.9 us; the launch traced here: 30.7 us
  Pallas kernels  28.9 us (94%)
  local copies, waits for them, and re-layouts  1.88 us (6%)
    pallas_call x1, Pallas kernels, shards(): pl.pallas_call(functools.partial(kernel, n_ctx, n_chan), out_shape=jax.Sh...  28.9 us
    unnamed x1, local copies, waits for them, and re-layouts  1.88 us

profile of v4, /device:TPU:1, one launch (start us, length us, event | category | flops | bytes accessed | tf_op | source)
XLA Modules:
  0.0 30.7 jit_solution(8663254985031019323)
XLA Ops:
  0.0 28.9 %shard_map.82 = bf16[128,2048]{1,0:T(8,128)(2,1)} custom-call(bf16[128,512]{1,0:T(8,128)(2,1)} %query_hbm.1, bf16[128,512]{1,0:T(8,128)(2,1)} %key_hbm.1, bf16[128,512]{1,0:T(8,128)(2,1)} %value_hbm.1, bf16[128,512]{1,0:T(8,128)(2,1)} %filter_hbm.1, f32[1,512]{1,0:T(1,128)} %bitcast.1, bf16[128,256]{1,0:T(8,128)(2,1)} %constant.4.clone.fwd_hbm, ...), custom_call_target="tpu_custom_call" | custom-call | tf_op jit(solution)/shard_map/pallas_call | solution.py:328
  28.9 1.9 %copy.10 = bf16[128,2048]{1,0:T(8,128)(2,1)} copy(bf16[128,2048]{1,0:T(8,128)(2,1)} %shard_map.82) | data formatting | bytes 1048576

commit v5 on v4

--- a/solution.py
+++ b/solution.py
@@ -13,7 +13,7 @@
 TILE = 8
 LANES = 128
 PIECES = 4
-AHEAD = 4
+AHEAD = 3
 W_PIECES = 4
 
 

time: 30.9 us -> 30.1 us (0.974)
  the two profiles are of different devices: /device:TPU:1 before, /device:TPU:0 now
where the time goes in v5:
time: 30.1 us; the launch traced here: 29.9 us
  Pallas kernels  28 us (93%)
  local copies, waits for them, and re-layouts  1.88 us (6%)
    pallas_call x1, Pallas kernels, shards(): pl.pallas_call(functools.partial(kernel, n_ctx, n_chan), out_shape=jax.Sh...  28 us
    unnamed x1, local copies, waits for them, and re-layouts  1.88 us

profile of v5, /device:TPU:0, one launch (start us, length us, event | category | flops | bytes accessed | tf_op | source)
XLA Modules:
  0.0 29.9 jit_solution(14618012241690196846)
XLA Ops:
  0.0 28.0 %shard_map.82 = bf16[128,2048]{1,0:T(8,128)(2,1)} custom-call(bf16[128,512]{1,0:T(8,128)(2,1)} %query_hbm.1, bf16[128,512]{1,0:T(8,128)(2,1)} %key_hbm.1, bf16[128,512]{1,0:T(8,128)(2,1)} %value_hbm.1, bf16[128,512]{1,0:T(8,128)(2,1)} %filter_hbm.1, f32[1,512]{1,0:T(1,128)} %bitcast.1, bf16[128,256]{1,0:T(8,128)(2,1)} %constant.4.clone.fwd_hbm, ...), custom_call_target="tpu_custom_call" | custom-call | tf_op jit(solution)/shard_map/pallas_call | solution.py:328
  28.0 1.9 %copy.10 = bf16[128,2048]{1,0:T(8,128)(2,1)} copy(bf16[128,2048]{1,0:T(8,128)(2,1)} %shard_map.82) | data formatting | bytes 1048576
